TPU v7x, 32 devices: a whole 2x2x4 slice. The times are simulated.
32 devices in a mesh: atlas: 4 (over y, x), row: 2 (over core), col: 4 (over z).
Axes of the slice: x: 2, y: 2, z: 4, core: 2. Of those that a mesh axis runs over, the one named last changes fastest.
Arguments:
- cells: bfloat16 [4, 64, 1024], P('atlas', None, 'row'), may hold values from -4 to 4
- support: bfloat16 [64, 16384], P(None, 'col'), may hold values from -4 to 4
Outputs:
- cell_dual: float32 [4, 1024], P('atlas', 'row')
- support_dual: float32 [4, 16384], P('atlas', 'col')
- new_support: float32 [64, 16384], P(None, 'col')
All inputs are finite; a program needn't handle non-finite values.
Results may differ from a plain program's by a relative error of at most 0.001.
Values sent between devices are 32-bit elements; how exact they have to be, the bound alone decides.
No kernel may reach another device: no remote copies, remote signals or barrier semaphores. Data moves between devices by JAX's collectives and lax.ppermute only.
A program may use at most 64 MiB of HBM per device.

v0:
```python
import jax
import jax.numpy as jnp
from jax import lax
from jax.sharding import PartitionSpec as P

ITERS = 2
blur = 0.1


def combined_all(value, axis, join):
    pieces = jax.tree.map(lambda part: lax.all_gather(part, axis), value)
    head = jax.tree.map(lambda part: part[0], pieces)
    tail = jax.tree.map(lambda part: part[1:], pieces)
    subtotal, _ = lax.scan(lambda subtotal, slab: (join(subtotal, slab), None), head, tail)
    return subtotal


def lse_pair(first, second):
    top_one, total_one = first
    top_two, total_two = second
    peak = jnp.maximum(top_one, top_two)
    return (peak, total_one * jnp.exp(top_one - peak) + total_two * jnp.exp(top_two - peak))


def shards(cells, support):
    points = cells[0]
    dims, rows = points.shape
    columns = support.shape[1]
    width_block = min(512, columns)
    count = columns // width_block
    points_wide = points.astype(jnp.float32)
    squares_x = jnp.sum(jnp.square(points_wide), axis=0)
    squares_y = jnp.sum(jnp.square(support.astype(jnp.float32)), axis=0)
    total_cells = rows * lax.axis_size("row")
    total_support = columns * lax.axis_size("col")
    atlases = lax.axis_size("atlas")

    def tile_cost(start):
        piece = lax.dynamic_slice_in_dim(support, start, width_block, 1)
        near = lax.dynamic_slice_in_dim(squares_y, start, width_block, 0)
        cross = lax.dot_general(
            points, piece, (((0,), (0,)), ((), ())), preferred_element_type=jnp.float32
        )
        return (squares_x[:, None] + near[None, :] - 2.0 * cross) / dims

    def row_step(dual_g):

        def row_visit(index, carry):
            top, total = carry
            start = index * width_block
            gpart = lax.dynamic_slice_in_dim(dual_g, start, width_block, 0)
            logits = (gpart[None, :] - tile_cost(start)) / blur
            peak = jnp.maximum(top, jnp.max(logits, axis=1))
            total = total * jnp.exp(top - peak) + jnp.sum(jnp.exp(logits - peak[:, None]), axis=1)
            return (peak, total)

        start_carry = (jnp.full((rows,), -jnp.inf, jnp.float32), jnp.zeros((rows,), jnp.float32))
        top, total = lax.fori_loop(0, count, row_visit, start_carry)
        top, total = combined_all((top, total), "col", lse_pair)
        return blur * jnp.log(1.0 / total_cells) - blur * (top + jnp.log(total))

    def column_step(dual_f):

        def column_visit(index, carry):
            top, total = carry
            start = index * width_block
            logits = (dual_f[:, None] - tile_cost(start)) / blur
            peak = jnp.max(logits, axis=0)
            mass = jnp.sum(jnp.exp(logits - peak[None, :]), axis=0)
            return (
                lax.dynamic_update_slice_in_dim(top, peak, start, 0),
                lax.dynamic_update_slice_in_dim(total, mass, start, 0),
            )

        start_carry = (jnp.zeros((columns,), jnp.float32), jnp.zeros((columns,), jnp.float32))
        top, total = lax.fori_loop(0, count, column_visit, start_carry)
        top, total = combined_all((top, total), "row", lse_pair)
        return blur * jnp.log(1.0 / total_support) - blur * (top + jnp.log(total))

    dual_g = jnp.zeros((columns,), jnp.float32)
    dual_f = jnp.zeros((rows,), jnp.float32)
    for step in range(ITERS):
        dual_f = row_step(dual_g)
        dual_g = column_step(dual_f)

    def positions_visit(index, summed):
        start = index * width_block
        gpart = lax.dynamic_slice_in_dim(dual_g, start, width_block, 0)
        plan = jnp.exp((dual_f[:, None] + gpart[None, :] - tile_cost(start)) / blur)
        moved = jnp.dot(points_wide, plan, precision=lax.Precision.HIGHEST) * total_support
        return lax.dynamic_update_slice_in_dim(summed, moved, start, 1)

    terms = lax.fori_loop(0, count, positions_visit, jnp.zeros((dims, columns), jnp.float32))
    summed = lax.psum(terms, ("atlas", "row"))
    updated = summed / atlases
    return (dual_f[None, :], dual_g[None, :], updated)


def solution(mesh):
    in_specs = (P("atlas", None, "row"), P(None, "col"))
    out_specs = (P("atlas", "row"), P("atlas", "col"), P(None, "col"))
    return jax.shard_map(shards, mesh=mesh, in_specs=in_specs, out_specs=out_specs, check_vma=False)
```

profile of v0, /device:TPU:0, one launch (start us, length us, event | category | flops | bytes accessed | tf_op | source)
XLA Modules:
  0.0 182.5 jit_solution(9270883459431666822)
XLA Ops:
  7.3 0.9 multiply_reduce_fusion.1
  8.2 1.2 multiply_reduce_fusion
  9.4 6.2 %while.114 = (s32[]{:T(128)}, f32[512]{0:T(512)S(1)}, f32[512]{0:T(512)S(1)}, f32[512]{0:T(512)S(1)}, f32[4096]{0:T(1024)S(1)}, /*index=5*/bf16[64,4096]{1,0:T(8...) while((s32[]{:T(128)}, f32[512]{0:T(512)S(1)}, ...), condition=%wide.region_5.0_spmd.clone, body=%wide.region_2.0_spmd.clone.sunk | while | flops 35916292 | bytes 2263222 | solution.py:58
  15.6 13.6 %all-gather.8 = f32[4,1,512]{2,1,0:T(1,128)S(1)} all-gather(f32[1,1,512]{2,1,0:T(1,128)S(1)} %bitcast.124), channel_id=2, replica_groups=mesh['atlas'=4,'row'=2,'col'=4] {'col'}, dimensions={0}, use_global_device_ids=true | all-gather | bytes 10240 | tf_op jit(solution)/shard_map/all_gather | solution.py:11
  29.3 0.6 copy-done.4
  29.9 11.9 %all-gather.9 = f32[4,1,512]{2,1,0:T(1,128)S(1)} all-gather(f32[1,1,512]{2,1,0:T(1,128)S(1)} %bitcast.134), channel_id=3, replica_groups=mesh['atlas'=4,'row'=2,'col'=4] {'col'}, dimensions={0}, use_global_device_ids=true | all-gather | bytes 10240 | tf_op jit(solution)/shard_map/all_gather | solution.py:11
  41.8 0.7 slice-done.3
  42.5 0.7 slice-done.2
  43.4 10.0 %while.110 = (s32[]{:T(128)}, f32[4096]{0:T(1024)S(1)}, f32[4096]{0:T(1024)S(1)}, f32[512]{0:T(512)S(1)}, f32[512]{0:T(512)S(1)}, /*index=5*/f32[4096]{0:T(1024)...) while((s32[]{:T(128)}, f32[4096]{0:T(1024)S(1)}, ...), condition=%wide.region_11.12_spmd, body=%wide.region_8.11_spmd.sunk | while | flops 35912708 | bytes 2252979 | solution.py:76
  43.5 0.5 fusion.78
  44.7 0.5 fusion.78
  46.0 0.5 fusion.78
  47.3 0.5 fusion.78
  48.5 0.5 fusion.78
  49.8 0.5 fusion.78
  51.0 0.5 fusion.78
  52.2 0.5 fusion.78
  53.4 1.8 all-gather.3
  55.2 1.8 all-gather.2
  57.0 6.8 %while.115 = (s32[]{:T(128)}, f32[512]{0:T(512)S(1)}, f32[512]{0:T(512)S(1)}, f32[4096]{0:T(1024)S(1)}, f32[512]{0:T(512)S(1)}, /*index=5*/f32[4096]{0:T(1024)S(...) while((s32[]{:T(128)}, f32[512]{0:T(512)S(1)}, ...), condition=%wide.region_15.16_spmd.clone, body=%wide.region_12.0_spmd.clone.sunk | while | flops 35916292 | bytes 2269378 | solution.py:58
  57.2 0.4 fusion.91
  58.1 0.5 fusion.91
  58.9 0.4 fusion.91
  60.6 0.4 fusion.91
  61.5 0.5 fusion.91
  63.9 11.9 %all-gather.10 = f32[4,1,512]{2,1,0:T(1,128)S(1)} all-gather(f32[1,1,512]{2,1,0:T(1,128)S(1)} %bitcast.123), channel_id=6, replica_groups=mesh['atlas'=4,'row'=2,'col'=4] {'col'}, dimensions={0}, use_global_device_ids=true | all-gather | bytes 10240 | tf_op jit(solution)/shard_map/all_gather | solution.py:11
  75.8 0.6 copy-done.3
  76.4 11.9 %all-gather.11 = f32[4,1,512]{2,1,0:T(1,128)S(1)} all-gather(f32[1,1,512]{2,1,0:T(1,128)S(1)} %bitcast.133), channel_id=7, replica_groups=mesh['atlas'=4,'row'=2,'col'=4] {'col'}, dimensions={0}, use_global_device_ids=true | all-gather | bytes 10240 | tf_op jit(solution)/shard_map/all_gather | solution.py:11
  88.3 0.6 copy-done.5
  88.9 0.7 slice-done.1
  89.6 0.7 slice-done.5
  90.3 0.7 slice-done.4
  91.2 10.0 %while.112 = (s32[]{:T(128)}, f32[4096]{0:T(1024)S(1)}, f32[4096]{0:T(1024)S(1)}, f32[512]{0:T(512)S(1)}, f32[512]{0:T(512)S(1)}, /*index=5*/f32[4096]{0:T(1024)...) while((s32[]{:T(128)}, f32[4096]{0:T(1024)S(1)}, ...), condition=%wide.region_21.22_spmd, body=%wide.region_18.0_spmd.sunk | while | flops 35912708 | bytes 2252979 | solution.py:76
  91.3 0.5 fusion.80
  92.6 0.5 fusion.80
  93.8 0.5 fusion.80
  95.1 0.5 fusion.80
  96.4 0.5 fusion.80
  97.6 0.5 fusion.80
  98.9 0.5 fusion.80
  100.1 0.5 fusion.80
  101.2 1.8 all-gather.7
  103.0 1.8 all-gather.6
  104.9 12.0 %while.113 = (s32[]{:T(128)}, f32[64,4096]{1,0:T(8,128)S(1)}, f32[512]{0:T(512)S(1)}, f32[4096]{0:T(1024)S(1)}, f32[512]{0:T(512)S(1)}, /*index=5*/f32[4096]{0:T...) while((s32[]{:T(128)}, f32[64,4096]{1,0:T(8,128)S(1)}, ...), condition=%wide.region_23.24_spmd, body=%wide.region_22.23_spmd.sunk | while | flops 236748800 | bytes 2506939 | solution.py:93
  105.1 0.5 fusion.85
  105.6 0.8 fusion.86
  106.6 0.5 fusion.85
  107.1 0.8 fusion.86
  108.1 0.5 fusion.85
  108.6 0.8 fusion.86
  109.6 0.5 fusion.85
  110.1 0.8 fusion.86
  111.1 0.5 fusion.85
  111.6 0.8 fusion.86
  112.6 0.5 fusion.85
  113.1 0.8 fusion.86
  114.1 0.5 fusion.85
  114.6 0.8 fusion.86
  115.6 0.5 fusion.85
  116.1 0.8 fusion.86
  116.9 0.6 copy-done.6
  117.9 0.7 multiply_subtract_fusion.1
  118.6 54.8 %all-reduce.2.cloned.1.call-done = f32[64,4096]{1,0:T(8,128)} async-done(((f32[64,4096]{1,0:T(8,128)}), f32[64,4096]{1,0:T(8,128)}) %all-reduce.2.cloned.1.call-update) | async-done | bytes 1048592 | tf_op jit(solution)/shard_map/psum | solution.py:94
  173.4 2.3 %broadcast_multiply_fusion = f32[64,4096]{1,0:T(8,128)} fusion(f32[64,4096]{1,0:T(8,128)} %all-reduce.2.cloned.1.call-done), kind=kLoop, calls=%fused_computation.61 | loop fusion | flops 262144 | bytes 2097152 | tf_op jit(solution)/shard_map/div | solution.py:95
  (232 shorter events, 25.1 us)
Async XLA Ops:
  7.2 2.2 %copy-start.1 = (bf16[64,4096]{1,0:T(8,128)(2,1)S(1)}, bf16[64,4096]{1,0:T(8,128)(2,1)}, u32[]{:S(2)}) copy-start(bf16[64,4096]{1,0:T(8,128)(2,1)} %param.17) | copy-start | bytes 1572868
  7.2 166.2 %all-reduce.2.cloned.1.call-start = ((), (), s32[]{:S(2)}) async-start(), calls=%async_computation | async-start | bytes 2097152 | tf_op jit(solution)/shard_map/psum | solution.py:94
  8.2 1.2 copy-start.2
  29.3 0.6 copy-start.4
  41.8 0.7 slice-start.3
  42.5 0.7 slice-start.2
  75.8 0.6 copy-start.3
  88.3 0.6 copy-start.5
  88.9 0.7 slice-start.1
  89.6 0.7 slice-start.5
  90.3 0.7 slice-start.4
  90.3 0.7 slice-start
  116.9 0.6 copy-start.6
  116.9 1.0 copy-start
Sparse Core Ops, SparseCore 0:
  118.0 55.2 all-reduce.1
where the time goes:
time: 183 us; the launch traced here: 182 us
  blocking collectives  56.7 us (31%)
  waiting for transfers between devices  54.8 us (30%)
  matrix products  25.1 us (14%)
  local copies, waits for them, and re-layouts  18.8 us (10%)
  between operations  14.2 us (8%)
  other arithmetic  12 us (7%)
    all_gather x8, blocking collectives, combined_all(): pieces = jax.tree.map(lambda part: lax.all_gather(part, axis), value)  56.7 us
    psum x1, waiting for transfers between devices, shards(): summed = lax.psum(terms, ('atlas', 'row'))  54.8 us
    dot_general x40, matrix products, tile_cost(): lax.dot_general(points, piece, (((0,), (0,)), ((), ())), preferred_elemen...  18.7 us
    dot_general x8, matrix products, positions_visit(): jnp.dot(points_wide, plan, precision=lax.Precision.HIGHEST) * total_support  6.37 us
    dynamic_update_slice x16, local copies, waits for them, and re-layouts, column_visit(): lax.dynamic_update_slice_in_dim(top, peak, start, 0)  4.3 us
    dynamic_update_slice x16, local copies, waits for them, and re-layouts, column_visit(): lax.dynamic_update_slice_in_dim(total, mass, start, 0)  3.85 us
  transfers between devices with their start and end apart: 1, of which 1 were waited for; matrix products, arithmetic and copies ran while one was open for 0% of the time, Pallas kernels for 0%

commit v1 on v0

--- a/solution.py
+++ b/solution.py
@@ -91,7 +91,7 @@
         return lax.dynamic_update_slice_in_dim(summed, moved, start, 1)
 
     terms = lax.fori_loop(0, count, positions_visit, jnp.zeros((dims, columns), jnp.float32))
-    summed = lax.psum(terms, ("atlas", "row"))
+    summed = lax.psum(lax.psum(terms, "row"), "atlas")
     updated = summed / atlases
     return (dual_f[None, :], dual_g[None, :], updated)
 

time: 183 us -> 202 us (1.10)
  waiting for transfers between devices: 54.8 us -> 74.2 us
    psum x1 -> x2, waiting for transfers between devices: 54.8 us -> 74.2 us  [shards(): summed = lax.psum(lax.psum(terms, 'row'), 'atlas')]
  transfers between devices with their start and end apart: 1 -> 2, of which waited for: 1 -> 2; matrix products, arithmetic and copies ran while one was open for 0% -> 0% of each run, Pallas kernels for 0% -> 0%
where the time goes in v1:
time: 202 us
  waiting for transfers between devices  74.2 us (37%)
  blocking collectives  56.7 us (28%)
  matrix products  25.1 us (12%)
  local copies, waits for them, and re-layouts  18.8 us (9%)
  between operations  14.2 us (7%)
  other arithmetic  12 us (6%)
    psum x2, waiting for transfers between devices, shards(): summed = lax.psum(lax.psum(terms, 'row'), 'atlas')  74.2 us
    all_gather x8, blocking collectives, combined_all(): pieces = jax.tree.map(lambda part: lax.all_gather(part, axis), value)  56.7 us
    dot_general x40, matrix products, tile_cost(): lax.dot_general(points, piece, (((0,), (0,)), ((), ())), preferred_elemen...  18.7 us
    dot_general x8, matrix products, positions_visit(): jnp.dot(points_wide, plan, precision=lax.Precision.HIGHEST) * total_support  6.37 us
    dynamic_update_slice x16, local copies, waits for them, and re-layouts, column_visit(): lax.dynamic_update_slice_in_dim(top, peak, start, 0)  4.3 us
  transfers between devices with their start and end apart: 2, of which 2 were waited for; matrix products, arithmetic and copies ran while one was open for 0% of the time, Pallas kernels for 0%

profile of v1, /device:TPU:0, one launch (start us, length us, event | category | flops | bytes accessed | tf_op | source)
XLA Modules:
  0.0 201.9 jit_solution(5671251769491468852)
XLA Ops:
  7.3 0.9 multiply_reduce_fusion.1
  8.2 1.2 multiply_reduce_fusion
  9.4 6.2 %while.114 = (s32[]{:T(128)}, f32[512]{0:T(512)S(1)}, f32[512]{0:T(512)S(1)}, f32[512]{0:T(512)S(1)}, f32[4096]{0:T(1024)S(1)}, /*index=5*/bf16[64,4096]{1,0:T(8...) while((s32[]{:T(128)}, f32[512]{0:T(512)S(1)}, ...), condition=%wide.region_5.0_spmd.clone, body=%wide.region_2.0_spmd.clone.sunk | while | flops 35916292 | bytes 2263222 | solution.py:58
  15.6 13.6 %all-gather.8 = f32[4,1,512]{2,1,0:T(1,128)S(1)} all-gather(f32[1,1,512]{2,1,0:T(1,128)S(1)} %bitcast.124), channel_id=2, replica_groups=mesh['atlas'=4,'row'=2,'col'=4] {'col'}, dimensions={0}, use_global_device_ids=true | all-gather | bytes 10240 | tf_op jit(solution)/shard_map/all_gather | solution.py:11
  29.3 0.6 copy-done.4
  29.9 11.9 %all-gather.9 = f32[4,1,512]{2,1,0:T(1,128)S(1)} all-gather(f32[1,1,512]{2,1,0:T(1,128)S(1)} %bitcast.134), channel_id=3, replica_groups=mesh['atlas'=4,'row'=2,'col'=4] {'col'}, dimensions={0}, use_global_device_ids=true | all-gather | bytes 10240 | tf_op jit(solution)/shard_map/all_gather | solution.py:11
  41.8 0.7 slice-done.3
  42.5 0.7 slice-done.2
  43.4 10.0 %while.110 = (s32[]{:T(128)}, f32[4096]{0:T(1024)S(1)}, f32[4096]{0:T(1024)S(1)}, f32[512]{0:T(512)S(1)}, f32[512]{0:T(512)S(1)}, /*index=5*/f32[4096]{0:T(1024)...) while((s32[]{:T(128)}, f32[4096]{0:T(1024)S(1)}, ...), condition=%wide.region_11.12_spmd, body=%wide.region_8.11_spmd.sunk | while | flops 35912708 | bytes 2252979 | solution.py:76
  43.5 0.5 fusion.78
  44.7 0.5 fusion.78
  46.0 0.5 fusion.78
  47.3 0.5 fusion.78
  48.5 0.5 fusion.78
  49.8 0.5 fusion.78
  51.0 0.5 fusion.78
  52.2 0.5 fusion.78
  53.4 1.8 all-gather.3
  55.2 1.8 all-gather.2
  57.0 6.8 %while.115 = (s32[]{:T(128)}, f32[512]{0:T(512)S(1)}, f32[512]{0:T(512)S(1)}, f32[4096]{0:T(1024)S(1)}, f32[512]{0:T(512)S(1)}, /*index=5*/f32[4096]{0:T(1024)S(...) while((s32[]{:T(128)}, f32[512]{0:T(512)S(1)}, ...), condition=%wide.region_15.16_spmd.clone, body=%wide.region_12.0_spmd.clone.sunk | while | flops 35916292 | bytes 2269378 | solution.py:58
  58.1 0.5 fusion.91
  58.9 0.4 fusion.91
  60.6 0.4 fusion.91
  61.5 0.5 fusion.91
  63.9 11.9 %all-gather.10 = f32[4,1,512]{2,1,0:T(1,128)S(1)} all-gather(f32[1,1,512]{2,1,0:T(1,128)S(1)} %bitcast.123), channel_id=6, replica_groups=mesh['atlas'=4,'row'=2,'col'=4] {'col'}, dimensions={0}, use_global_device_ids=true | all-gather | bytes 10240 | tf_op jit(solution)/shard_map/all_gather | solution.py:11
  75.8 0.6 copy-done.3
  76.4 11.9 %all-gather.11 = f32[4,1,512]{2,1,0:T(1,128)S(1)} all-gather(f32[1,1,512]{2,1,0:T(1,128)S(1)} %bitcast.133), channel_id=7, replica_groups=mesh['atlas'=4,'row'=2,'col'=4] {'col'}, dimensions={0}, use_global_device_ids=true | all-gather | bytes 10240 | tf_op jit(solution)/shard_map/all_gather | solution.py:11
  88.3 0.6 copy-done.5
  88.9 0.7 slice-done.1
  89.6 0.7 slice-done.5
  90.3 0.7 slice-done.4
  91.2 10.0 %while.112 = (s32[]{:T(128)}, f32[4096]{0:T(1024)S(1)}, f32[4096]{0:T(1024)S(1)}, f32[512]{0:T(512)S(1)}, f32[512]{0:T(512)S(1)}, /*index=5*/f32[4096]{0:T(1024)...) while((s32[]{:T(128)}, f32[4096]{0:T(1024)S(1)}, ...), condition=%wide.region_21.22_spmd, body=%wide.region_18.0_spmd.sunk | while | flops 35912708 | bytes 2252979 | solution.py:76
  91.3 0.5 fusion.80
  92.6 0.5 fusion.80
  93.8 0.5 fusion.80
  95.1 0.5 fusion.80
  96.4 0.5 fusion.80
  97.6 0.5 fusion.80
  98.9 0.5 fusion.80
  100.1 0.5 fusion.80
  101.2 1.8 all-gather.7
  103.0 1.8 all-gather.6
  104.9 12.0 %while.113 = (s32[]{:T(128)}, f32[64,4096]{1,0:T(8,128)S(1)}, f32[512]{0:T(512)S(1)}, f32[4096]{0:T(1024)S(1)}, f32[512]{0:T(512)S(1)}, /*index=5*/f32[4096]{0:T...) while((s32[]{:T(128)}, f32[64,4096]{1,0:T(8,128)S(1)}, ...), condition=%wide.region_23.24_spmd, body=%wide.region_22.23_spmd.sunk | while | flops 236748800 | bytes 2506939 | solution.py:93
  105.1 0.5 fusion.85
  105.6 0.8 fusion.86
  106.6 0.5 fusion.85
  107.1 0.8 fusion.86
  108.1 0.5 fusion.85
  108.6 0.8 fusion.86
  109.6 0.5 fusion.85
  110.1 0.8 fusion.86
  111.1 0.5 fusion.85
  111.6 0.8 fusion.86
  112.6 0.5 fusion.85
  113.1 0.8 fusion.86
  114.1 0.5 fusion.85
  114.6 0.8 fusion.86
  115.6 0.5 fusion.85
  116.1 0.8 fusion.86
  116.9 0.6 copy-done.6
  118.0 18.1 %all-reduce.3.cloned.1.call-done = f32[64,4096]{1,0:T(8,128)} async-done(((f32[64,4096]{1,0:T(8,128)}), f32[64,4096]{1,0:T(8,128)}) %all-reduce.3.cloned.1.call-update) | async-done | bytes 1048592 | tf_op jit(solution)/shard_map/psum | solution.py:94
  136.1 0.7 multiply_subtract_fusion.1
  136.8 56.0 %all-reduce.5.cloned.1.call-done = f32[64,4096]{1,0:T(8,128)} async-done(((f32[64,4096]{1,0:T(8,128)}), f32[64,4096]{1,0:T(8,128)}) %all-reduce.5.cloned.1.call-update) | async-done | bytes 1048592 | tf_op jit(solution)/shard_map/psum | solution.py:94
  192.8 2.3 %broadcast_multiply_fusion = f32[64,4096]{1,0:T(8,128)} fusion(f32[64,4096]{1,0:T(8,128)} %all-reduce.5.cloned.1.call-done), kind=kLoop, calls=%fused_computation.61 | loop fusion | flops 262144 | bytes 2097152 | tf_op jit(solution)/shard_map/div | solution.py:95
  (235 shorter events, 25.6 us)
Async XLA Ops:
  7.2 2.2 %copy-start.1 = (bf16[64,4096]{1,0:T(8,128)(2,1)S(1)}, bf16[64,4096]{1,0:T(8,128)(2,1)}, u32[]{:S(2)}) copy-start(bf16[64,4096]{1,0:T(8,128)(2,1)} %param.17) | copy-start | bytes 1572868
  7.2 128.9 %all-reduce.3.cloned.1.call-start = ((), (), s32[]{:S(2)}) async-start(), calls=%async_computation | async-start | bytes 2097152 | tf_op jit(solution)/shard_map/psum | solution.py:94
  8.2 1.2 copy-start.2
  29.3 0.6 copy-start.4
  41.8 0.7 slice-start.3
  42.5 0.7 slice-start.2
  75.8 0.6 copy-start.3
  88.3 0.6 copy-start.5
  88.9 0.7 slice-start.1
  89.6 0.7 slice-start.5
  90.3 0.7 slice-start.4
  90.3 0.7 slice-start
  116.9 0.6 copy-start.6
  116.9 1.0 copy-start
  117.9 74.9 %all-reduce.5.cloned.1.call-start = ((), (), s32[]{:S(2)}) async-start(), calls=%async_computation.1 | async-start | bytes 2097152 | tf_op jit(solution)/shard_map/psum | solution.py:94
Sparse Core Ops, SparseCore 0:
  118.0 17.9 all-reduce.2
  139.1 53.6 all-reduce.4
